TPU v7x, 32 devices: a whole 2x2x4 slice. The times are simulated.
32 devices in a mesh: grp: 2 (over x), ctx: 16 (over z, y, core).
Axes of the slice: x: 2, y: 2, z: 4, core: 2. Of those that a mesh axis runs over, the one named last changes fastest.
Arguments:
- queries: bfloat16 [4096, 4096], P(('grp', 'ctx')), parts along dimension 0, may hold values from -6 to 6
- keys_values: bfloat16 [4096, 2048], P(('grp', 'ctx')), parts along dimension 0, may hold values from -6 to 6
- depth_kernel: float32 [8, 2048], replicated, may hold values from -2.1 to 2.1
- point_weight: bfloat16 [2, 1024, 1024], replicated, may hold values from -0.1875 to 0.1875
- page_table: int32 [64], P('grp'), parts along dimension 0, may hold values from 0 to 31, each once
- doc_lengths: int32 [8], P('grp'), parts along dimension 0, may hold values from 1 to 1024, 2048 in all
Outputs:
- attended: bfloat16 [4096, 4096], P(('grp', 'ctx')), parts along dimension 0
- kv_tier: bfloat16 [1024, 2048], P(('grp', 'ctx')), parts along dimension 0
There are 2 independent parts, one for each index of `grp`. A program takes and returns all parts, laid end to end along the dimension named above; an argument that names none is the same for every part. Nothing has to cross between parts.
Inputs may be any that keep to these rules, and one draw needn't show every extreme that they name: Slot s, the s-th page of the shards of queries and keys_values, holds logical page page_table[s]; every page stands in exactly one slot. `doc_lengths`: the documents lie end to end and cover the sequence.
All inputs are finite; a program needn't handle non-finite values.
Results may differ from a plain program's by a relative error of at most 0.0061.
Values may be sent and summed in bfloat16 or wider, within the bound.
A program may use at most 64 MiB of HBM per device.

v0:
```python
import jax
import jax.numpy as jnp
from jax import lax
from jax.sharding import PartitionSpec as P

KVH = 8
HD = 128
QH = 32
KERNEL = 8
STRIDE = 4
PAGE = 64


SCORE_SCALE = 6.0


def unit_rows(block, head_count):
    row_count = block.shape[0]
    pieces = block.astype(jnp.float32).reshape(row_count, head_count, -1)
    factor = lax.rsqrt(jnp.mean(pieces * pieces, axis=2, keepdims=True) + 1e-06)
    return (pieces * factor).astype(jnp.bfloat16)


def shards(queries, keys_values, depth_kernel, point_weight, page_table, doc_lengths):
    rows_here = keys_values.shape[0]
    full_width = keys_values.shape[1]
    kv_width = full_width // 2
    slots_here = rows_here // PAGE
    rows_page = PAGE // STRIDE
    group_heads = QH // KVH
    total_pages = page_table.shape[0]
    device = lax.axis_index("ctx")
    my_slots = device * slots_here + jnp.arange(slots_here, dtype=jnp.int32)
    my_pages = jnp.take(page_table, my_slots)
    following = my_pages + 1
    matches = page_table[None, :] == following[:, None]
    succ_slot = jnp.sum(
        jnp.where(matches, jnp.arange(total_pages, dtype=jnp.int32)[None, :], 0), axis=1
    )
    has_next = following < total_pages
    local_pages = keys_values.reshape(slots_here, PAGE, full_width)
    blocks = local_pages.astype(jnp.float32).reshape(slots_here, rows_page, STRIDE, full_width)
    first_half = sum((blocks[:, :, offset, :] * depth_kernel[offset] for offset in range(STRIDE)))
    inner_half = sum(
        (blocks[:, 1:, offset, :] * depth_kernel[STRIDE + offset] for offset in range(STRIDE))
    )
    edge_rows = local_pages[:, : KERNEL - STRIDE, :]
    gathered = lax.all_gather(edge_rows, "ctx", axis=0, tiled=True)
    next_rows = jnp.take(gathered, succ_slot, axis=0).astype(jnp.float32)
    tail_terms = sum(
        (next_rows[:, offset, :] * depth_kernel[STRIDE + offset] for offset in range(STRIDE))
    )
    tail_terms = jnp.where(has_next[:, None], tail_terms, 0.0)
    second_half = jnp.concatenate([inner_half, tail_terms[:, None, :]], axis=1)
    depthwise = (
        (first_half + second_half).astype(jnp.bfloat16).reshape(slots_here * rows_page, full_width)
    )
    key_part = jnp.dot(depthwise[:, :kv_width], point_weight[0], preferred_element_type=jnp.float32)
    value_part = jnp.dot(
        depthwise[:, kv_width:], point_weight[1], preferred_element_type=jnp.float32
    )
    compressed = jnp.concatenate([key_part, value_part], axis=1).astype(jnp.bfloat16)
    position = (my_pages[:, None] * PAGE + jnp.arange(PAGE, dtype=jnp.int32)[None, :]).reshape(
        rows_here
    )
    doc_ends = jnp.cumsum(doc_lengths)
    doc_start = jnp.sum(
        jnp.where(doc_ends[None, :] <= position[:, None], doc_lengths[None, :], 0), axis=1
    )
    query_unit = unit_rows(queries, QH).reshape(rows_here, KVH, group_heads, HD)
    own_unit = unit_rows(keys_values[:, :kv_width], KVH)
    own_value = keys_values[:, kv_width:].reshape(rows_here, KVH, HD).astype(jnp.float32)
    own_score = jnp.einsum(
        "tkgd,tkd->tkg", query_unit, own_unit, preferred_element_type=jnp.float32
    )
    own_weight = jnp.exp(SCORE_SCALE / HD * own_score)
    initial = (own_weight[..., None] * own_value[:, :, None, :], own_weight)

    def add_block(state_pair, block_rows, first_row):
        mixture, weight_sum = state_pair
        row_count = block_rows.shape[0]
        row_index = first_row + jnp.arange(row_count, dtype=jnp.int32)
        slot_index = row_index // rows_page
        logical = jnp.take(page_table, slot_index) * rows_page + row_index % rows_page
        row_start = STRIDE * logical
        key_unit = unit_rows(block_rows[:, :kv_width], KVH)
        value_rows = block_rows[:, kv_width:].reshape(row_count, KVH, HD)
        scores = jnp.einsum(
            "tkgd,rkd->tkgr", query_unit, key_unit, preferred_element_type=jnp.float32
        )
        visible = (row_start[None, :] >= doc_start[:, None]) & (
            row_start[None, :] + KERNEL - 1 < position[:, None]
        )
        weights = jnp.where(visible[:, None, None, :], jnp.exp(SCORE_SCALE / HD * scores), 0.0)
        weights_low = weights.astype(jnp.bfloat16)
        mixture = mixture + jnp.einsum(
            "tkgr,rkd->tkgd", weights_low, value_rows, preferred_element_type=jnp.float32
        )
        weight_sum = weight_sum + jnp.sum(weights, axis=3)
        return (mixture, weight_sum)

    whole_tier = lax.all_gather(compressed, "ctx", axis=0, tiled=True)
    row_count = whole_tier.shape[0]
    shard_rows = compressed.shape[0]
    shard_count = row_count // shard_rows
    group_size = max((size for size in range(1, 17) if shard_count % size == 0))
    step_rows = shard_rows * group_size
    turn_count = row_count // step_rows

    def one_turn(index_turn, inner_pair):
        block_rows = lax.dynamic_slice_in_dim(whole_tier, index_turn * step_rows, step_rows, 0)
        return add_block(inner_pair, block_rows, 0 + index_turn * step_rows)

    mixture, weight_sum = lax.fori_loop(0, turn_count, one_turn, initial)
    attended = (mixture / weight_sum[..., None]).reshape(rows_here, QH * HD).astype(jnp.bfloat16)
    return (attended, compressed)


def solution(mesh):
    placed = (P(("grp", "ctx"), None), P(("grp", "ctx"), None), P(), P(), P("grp"), P("grp"))
    return jax.shard_map(
        shards,
        mesh=mesh,
        in_specs=placed,
        out_specs=(P(("grp", "ctx"), None), P(("grp", "ctx"), None)),
        check_vma=False,
    )
```

profile of v0, /device:TPU:1, one launch (start us, length us, event | category | flops | bytes accessed | tf_op | source)
XLA Modules:
  0.0 102.3 jit_solution(5705598395568139052)
XLA Ops:
  7.2 1.3 %gather_fusion = s32[2]{0:T(128)S(1)} fusion(s32[32]{0:T(128)} %param.10, s32[1024]{0:T(1024)S(1)} %pad_clamp_fusion.1), kind=kCustom, calls=%fused_computation | custom fusion | bytes 24 | tf_op jit(solution)/shard_map/jit(_take)/gather | solution.py:34
  8.6 0.8 fusion.55
  9.4 1.4 %reshape.367 = f32[2,16,4,2048]{3,2,1,0:T(4,128)S(1)} reshape(bf16[128,2048]{1,0:T(8,128)(2,1)} %param.7) | data formatting | bytes 1572864 | tf_op jit(solution)/shard_map/convert_element_type | solution.py:42
  10.8 0.8 fusion.63
  12.7 0.9 slice.167
  13.5 24.5 %all_gather.6 = bf16[32,4,2048]{2,1,0:T(4,128)(2,1)S(1)} all-gather(bf16[2,4,2048]{2,1,0:T(4,128)(2,1)S(1)} %slice.167), channel_id=1, replica_groups=mesh['grp'=2,'ctx'=16] {'ctx'}, dimensions={0}, use_global_device_ids=true | all-gather | bytes 557056 | tf_op jit(solution)/shard_map/all_gather | solution.py:48
  39.7 2.2 %fusion.21 = bf16[32,1024]{1,0:T(8,128)(2,1)S(1)} fusion(bf16[2,1024,1024]{2,1,0:T(8,128)(2,1)} %param.9, bf16[32,2048]{1,0:T(8,128)(2,1)S(1)} %fusion.33), kind=kOutput, calls=%fused_computation.25 | convolution fusion | flops 67141632 | bytes 2228224 | tf_op jit(solution)/shard_map/dot_general | solution.py:59
  43.5 1.9 %reshape.355 = f32[128,8,4,128]{3,2,1,0:T(4,128)S(1)} reshape(bf16[128,4096]{1,0:T(8,128)(2,1)S(1)} %copy-done.1) | data formatting | bytes 3145728 | tf_op jit(solution)/shard_map/reshape | solution.py:19
  45.6 1.7 %copy.154 = f32[16,8,32,128]{3,2,1,0:T(8,128)} copy(f32[16,8,32,128]{3,1,2,0:T(8,128)S(1)} %multiply_bitcast_fusion) | data formatting | bytes 4194304
  47.3 2.3 %reduce_sum.58 = f32[128,32]{1,0:T(8,128)S(1)} reduce(f32[128,32,128]{2,1,0:T(8,128)} %bitcast.153, f32[]{:T(128)} %constant.114.clone.1), dimensions={2}, to_apply=%region_0.1 | reduce | flops 520192 | bytes 2113540 | tf_op jit(solution)/shard_map/reduce_sum | solution.py:20
  50.5 1.3 %fusion.13 = bf16[128,8,4,128]{3,0,2,1:T(8,128)(2,1)S(1)} fusion(f32[128,8,4,128]{3,2,1,0:T(4,128)S(1)} %reshape.355, f32[128,8,4]{0,2,1:T(4,128)S(1)} %bitcast.167), kind=kLoop, calls=%fused_computation.17 | loop fusion | flops 1048576 | bytes 3162112 | tf_op jit(solution)/shard_map/convert_element_type | solution.py:21
  51.9 1.0 copy-done.3
  52.8 1.3 %fusion.27 = f32[128,8,1,4]{3,2,1,0:T(1,128)S(1)} fusion(bf16[128,8,4,128]{3,0,2,1:T(8,128)(2,1)S(1)} %fusion.13, bf16[128,8,128,1]{2,1,0,3:T(8,128)(2,1)S(1)} %fusion.30), kind=kOutput, calls=%fused_computation.29 | convolution fusion | flops 1048576 | bytes 1327104 | tf_op jit(solution)/shard_map/tkgd,tkd->tkg/dot_general | solution.py:73
  54.4 1.0 %copy.146 = f32[128,1024]{0,1:T(8,128)} copy(f32[128,1024]{1,0:T(8,128)S(1)} %get-tuple-element.65) | data formatting | bytes 1048576 | tf_op jit(solution)/shard_map/convert_element_type | solution.py:72
  57.2 4.5 %compare_select_fusion.1 = s32[512,1]{0,1:T(1,128)S(1)} fusion(s32[]{:T(128)} %bitcast.51, s32[]{:T(128)} %bitcast.52, s32[]{:T(128)} %bitcast.53, s32[]{:T(128)} %bitcast.54, s32[]{:T(128)} %bitcast.55, s32[]{:T(128)} %bitcast.57, s32[]{:T(128)} %bitcast.56), kind=kLoop, calls=%fused_computation.97 | loop fusion | flops 11776 | bytes 2076 | tf_op jit(solution)/shard_map/while/body/eval_jaxpr/jit(_take)/gather | solution.py:84
  62.5 15.5 %broadcast_add_fusion = (s32[512]{0:T(512)S(1)}, s32[512]{0:T(512)S(1)}) fusion(pred[512]{0:T(512)(128)(4,1)S(1)} %compare_reduce_fusion, pred[512]{0:T(512)(128)(4,1)S(1)} %compare_reduce_fusion.1, pred[512]{0:T(512)(128)(4,1)S(1)} %compare_reduce_fusion.2, pred[512]{0:T(512)(128)(4,1)S(1)} %compare_reduce_fusion.3, ...), kind=kLoop, calls=%fused_computation.135 | loop fusion | flops 24576 | bytes 19044 | tf_op jit(solution)/shard_map/while/body/eval_jaxpr/sub | solution.py:92
  78.2 3.9 %all-gather.2.cloned.1.call-done = bf16[512,2048]{1,0:T(8,128)(2,1)} async-done(((bf16[32,2048]{1,0:T(8,128)(2,1)}), bf16[512,2048]{1,0:T(8,128)(2,1)}) %all-gather.2.cloned.1.call-update) | async-done | bytes 2097168 | tf_op jit(solution)/shard_map/all_gather | solution.py:102
  82.1 3.1 %convert_bitcast_fusion = (f32[64,8,8,128]{3,1,2,0:T(8,128)}, bf16[512,1024]{1,0:T(8,128)(2,1)S(1)}) fusion(bf16[512,2048]{1,0:T(8,128)(2,1)} %all-gather.2.cloned.1.call-done), kind=kLoop, calls=%fused_computation.18 | loop fusion | flops 524288 | bytes 5242880
  85.3 1.3 %copy.147 = bf16[512,1024]{0,1:T(8,128)(2,1)} copy(bf16[512,1024]{1,0:T(8,128)(2,1)S(1)} %get-tuple-element.56) | data formatting | bytes 2097152 | tf_op jit(solution)/shard_map/while/body/eval_jaxpr/reshape | solution.py:87
  86.6 2.1 %copy.156 = f32[64,8,8,128]{3,2,1,0:T(8,128)S(1)} copy(f32[64,8,8,128]{3,1,2,0:T(8,128)} %get-tuple-element.55) | data formatting | bytes 4194304
  89.5 0.9 fusion.24
  90.5 1.8 %fusion = (f32[128,8,4]{0,2,1:T(4,128)S(1)}, f32[8,512,128,4]{2,1,3,0:T(8,128)S(1)}) fusion(pred[128,512]{0,1:T(8,128)(4,1)S(1)} %compare_and_fusion, bf16[128,8,4,128]{3,0,2,1:T(8,128)(2,1)S(1)} %copy-done.4, bf16[512,8,128,1]{2,1,0,3:T(8,128)(2,1)S(1)} %fusion.24), kind=kOutput, calls=%fused_computation.3 | convolution fusion | flops 543158272 | bytes 10567680 | tf_op jit(solution)/shard_map/while/body/eval_jaxpr/tkgd,rkd->tkgr/dot_general | solution.py:88
  92.3 1.7 %fusion.8 = bf16[128,8,4,128]{0,3,2,1:T(8,128)(2,1)S(1)} fusion(bf16[512,8,128,1]{0,2,3,1:T(8,128)(2,1)S(1)} %bitcast.156, f32[8,512,128,4]{2,1,3,0:T(8,128)S(1)} %get-tuple-element.110, pred[128,512]{0,1:T(8,128)(4,1)S(1)} %compare_and_fusion, f32[128,8,4]{0,2,1:T(4,128)S(1)} %get-tuple-element.76, f32[128,8,128]{0,2,1:T(8,128)S(1)} %bitcast.158, ...), kind=kOutput, calls=%fused_computation.11 | convolution fusion | flops 545259520 | bytes 11108352 | tf_op jit(solution)/shard_map/while/body/eval_jaxpr/tkgr,rkd->tkgd/dot_general | solution.py:96
  94.1 1.3 %copy.139 = bf16[128,4096]{1,0:T(8,128)(2,1)} copy(bf16[128,4096]{0,1:T(8,128)(2,1)S(1)} %bitcast.157) | data formatting | bytes 2097152
  (93 shorter events, 9.5 us)
Async XLA Ops:
  7.2 75.0 %all-gather.2.cloned.1.call-start = ((), (), s32[]{:S(2)}) async-start(), calls=%async_computation | async-start | bytes 2228224 | tf_op jit(solution)/shard_map/all_gather | solution.py:102
  11.6 26.4 %copy-start.7 = (f32[8,2048]{1,0:T(8,128)S(1)}, f32[8,2048]{1,0:T(8,128)}, u32[]{:S(2)}) copy-start(f32[8,2048]{1,0:T(8,128)} %param.8) | copy-start | bytes 196612
  39.4 2.8 %copy-start.9 = (bf16[2,1024,1024]{2,1,0:T(8,128)(2,1)S(1)}, bf16[2,1024,1024]{2,1,0:T(8,128)(2,1)}, u32[]{:S(2)}) copy-start(bf16[2,1024,1024]{2,1,0:T(8,128)(2,1)} %param.9) | copy-start | bytes 12582916
  39.7 3.9 %copy-start.1 = (bf16[128,4096]{1,0:T(8,128)(2,1)S(1)}, bf16[128,4096]{1,0:T(8,128)(2,1)}, u32[]{:S(2)}) copy-start(bf16[128,4096]{1,0:T(8,128)(2,1)} %param.6) | copy-start | bytes 3145732
  47.3 2.4 %copy-start.2 = (bf16[128,2048]{1,0:T(8,128)(2,1)S(1)}, bf16[128,2048]{1,0:T(8,128)(2,1)}, u32[]{:S(2)}) copy-start(bf16[128,2048]{1,0:T(8,128)(2,1)} %param.7) | copy-start | bytes 1572868
  51.9 1.0 copy-start.3
  52.8 2.6 %copy-start.8 = (s32[4]{0:T(128)S(1)}, s32[4]{0:T(128)}, u32[]{:S(2)}) copy-start(s32[4]{0:T(128)} %param.11) | copy-start | bytes 52
  52.8 3.7 %copy-start = (s32[32]{0:T(128)S(1)}, s32[32]{0:T(128)}, u32[]{:S(2)}) copy-start(s32[32]{0:T(128)} %param.10) | copy-start | bytes 388
  89.3 1.2 %copy-start.4 = (bf16[128,8,4,128]{3,0,2,1:T(8,128)(2,1)S(1)}, bf16[128,8,4,128]{3,0,2,1:T(8,128)(2,1)}, u32[]{:S(2)}) copy-start(bf16[128,8,4,128]{3,0,2,1:T(8,128)(2,1)} %copy-done.3) | copy-start | bytes 3145732
  90.5 1.8 %copy-start.5 = (bf16[512,1024]{0,1:T(8,128)(2,1)S(1)}, bf16[512,1024]{0,1:T(8,128)(2,1)}, u32[]{:S(2)}) copy-start(bf16[512,1024]{0,1:T(8,128)(2,1)} %copy.147) | copy-start | bytes 3145732
  90.5 1.8 %copy-start.6 = (f32[128,1024]{0,1:T(8,128)S(1)}, f32[128,1024]{0,1:T(8,128)}, u32[]{:S(2)}) copy-start(f32[128,1024]{0,1:T(8,128)} %copy.146) | copy-start | bytes 1572868
Sparse Core Ops, SparseCore 0:
  43.5 38.5 all-gather.1
where the time goes:
time: 103 us; the launch traced here: 102 us
  other arithmetic  32.8 us (32%)
  blocking collectives  24.5 us (24%)
  local copies, waits for them, and re-layouts  19.2 us (19%)
  between operations  14.4 us (14%)
  matrix products  7.46 us (7%)
  waiting for transfers between devices  3.93 us (4%)
    all_gather x1, blocking collectives, shards(): gathered = lax.all_gather(edge_rows, 'ctx', axis=0, tiled=True)  24.5 us
    sub x1, other arithmetic, add_block(): row_start[None, :] + KERNEL - 1 < position[:, None]  15.5 us
    unnamed x28, local copies, waits for them, and re-layouts  6.9 us
    gather x26, other arithmetic, add_block(): jnp.take(page_table, slot_index) * rows_page + row_index % rows_page  5.33 us
    all_gather x1, waiting for transfers between devices, shards(): whole_tier = lax.all_gather(compressed, 'ctx', axis=0, tiled=True)  3.92 us
    unnamed x2, other arithmetic  3.37 us
    reduce_sum x3, other arithmetic, unit_rows(): factor = lax.rsqrt(jnp.mean(pieces * pieces, axis=2, keepdims=True) + 1e-06)  3.12 us
    convert_element_type x3, other arithmetic, unit_rows(): return (pieces * factor).astype(jnp.bfloat16)  2.4 us
  transfers between devices with their start and end apart: 1, of which 1 were waited for; matrix products, arithmetic and copies ran while one was open for 33% of the time, Pallas kernels for 0%

commit v1 on v0

v1 whole, which is shorter than its diff:
```python
import functools
import math
import jax
import jax.numpy as jnp
from jax import lax
from jax.experimental import pallas as pl
from jax.experimental.pallas import tpu as pltpu
from jax.sharding import PartitionSpec as P

KVH = 8
HD = 128
QH = 32
GROUP = QH // KVH
KERNEL = 8
STRIDE = 4
PAGE = 64
SCORE_SCALE = 6.0
EXP2_SCALE = SCORE_SCALE / HD * math.log2(math.e)
KV = KVH * HD
CR = PAGE // STRIDE
SLOTS = 2
ROWS = SLOTS * CR
TOK = SLOTS * PAGE
CHUNK_BLOCKS = 8
MESH = pl.DeviceIdType.MESH


def unit(x):
    return x * lax.rsqrt(jnp.mean(x * x, axis=1, keepdims=True) + 1e-06)


class Spread:
    def __init__(self, buf, z_send, z_recv, y_send, y_recv, c_send, c_recv, steps):
        self.buf, self.steps = buf, steps
        self.sems = dict(z=(z_send, z_recv), y=(y_send, y_recv), c=(c_send, c_recv))
        me = lax.axis_index("ctx")
        self.c = lax.rem(me, 2)
        self.y = lax.rem(me // 2, 2)
        self.z = me // 4

    def index(self, z, y, c):
        return (z * 2 + y) * 2 + c

    def origin(self, k, y, c):
        return self.index(lax.rem(self.z + self.steps - k, self.steps), y, c)

    def copy(self, kind, i, origin, target):
        send, recv = self.sems[kind]
        return pltpu.make_async_remote_copy(
            src_ref=self.buf.at[origin], dst_ref=self.buf.at[origin], send_sem=send.at[i],
            recv_sem=recv.at[i], device_id={"ctx": target}, device_id_type=MESH)

    def z_target(self, k):
        return self.index(lax.rem(self.z + k, self.steps), self.y, self.c)

    def z_out(self, k):
        return self.copy("z", k, self.origin(0, self.y, self.c), self.z_target(k))

    def z_in(self, k):
        return self.copy("z", k, self.origin(k, self.y, self.c), self.z_target(k))

    def y_out(self, k):
        return self.copy("y", k, self.origin(k, self.y, self.c), self.index(self.z, 1 - self.y, self.c))

    def y_in(self, k):
        return self.copy("y", k, self.origin(k, 1 - self.y, self.c), self.index(self.z, 1 - self.y, self.c))

    def c_out(self, j):
        y = self.y if j < self.steps else 1 - self.y
        return self.copy("c", j, self.origin(j % self.steps, y, self.c), self.index(self.z, self.y, 1 - self.c))

    def c_in(self, j):
        y = self.y if j < self.steps else 1 - self.y
        return self.copy("c", j, self.origin(j % self.steps, y, 1 - self.c), self.index(self.z, self.y, 1 - self.c))

    def begin(self):
        self.y_out(0).start()
        for k in range(1, self.steps):
            self.z_out(k).start()
        self.c_out(0).start()

    def relay_z(self, k):
        self.z_in(k).wait_recv()
        self.y_out(k).start()
        self.c_out(k).start()

    def relay_y(self, k):
        self.y_in(k).wait_recv()
        self.c_out(self.steps + k).start()

    def wait_c(self, j):
        self.c_in(j).wait_recv()

    def finish(self):
        for k in range(1, self.steps):
            self.z_out(k).wait_send()
        for k in range(self.steps):
            self.y_out(k).wait_send()
        for j in range(2 * self.steps):
            self.c_out(j).wait_send()


def kernel(n, pages, q_hbm, kv_ref, dk_ref, w_hbm, pt_ref, dl_ref, att_ref, tier_ref,
           q_ref, w_ref, kvf, edges, blocks, own, qn, acc, den, tails, tails_comp, keys,
           load_sem, ez_s, ez_r, ey_s, ey_r, ec_s, ec_r, mz_s, mz_r, my_s, my_r, mc_s, mc_r):
    steps = n // 4
    me = lax.axis_index("ctx")
    load_w = pltpu.make_async_copy(w_hbm, w_ref, load_sem.at[0])
    load_q = pltpu.make_async_copy(q_hbm, q_ref, load_sem.at[1])
    load_w.start()
    load_q.start()
    edge = Spread(edges, ez_s, ez_r, ey_s, ey_r, ec_s, ec_r, steps)
    main = Spread(blocks, mz_s, mz_r, my_s, my_r, mc_s, mc_r, steps)

    barrier = pltpu.get_barrier_semaphore()
    for k in range(1, steps):
        pl.semaphore_signal(barrier, inc=1, device_id={"ctx": edge.z_target(k)}, device_id_type=MESH)
    pl.semaphore_signal(barrier, inc=1, device_id={"ctx": edge.index(edge.z, 1 - edge.y, edge.c)}, device_id_type=MESH)
    pl.semaphore_signal(barrier, inc=1, device_id={"ctx": edge.index(edge.z, edge.y, 1 - edge.c)}, device_id_type=MESH)

    firsts, seconds = [], []
    for t in range(2 * KVH):
        cols = slice(t * HD, (t + 1) * HD)
        kvf[t] = kv_ref[:, cols].astype(jnp.float32)
        first = jnp.zeros((ROWS, HD), jnp.float32)
        second = jnp.zeros((ROWS, HD), jnp.float32)
        for o in range(STRIDE):
            x = kvf[t, pl.ds(o, ROWS, stride=STRIDE), :]
            first = first + x * dk_ref[o:o + 1, cols]
            second = second + x * dk_ref[STRIDE + o:STRIDE + o + 1, cols]
        firsts.append(first)
        seconds.append(second)
    first = jnp.concatenate(firsts, axis=1)
    second = jnp.concatenate(seconds, axis=1)
    for s in range(SLOTS):
        last, head = s * CR + CR - 1, s * CR
        for half in range(2):
            cols = slice(half * KV, (half + 1) * KV)
            edges[me, 2 * s + half:2 * s + half + 1, :] = first[last:last + 1, cols]
            edges[me, 4 + 2 * s + half:5 + 2 * s + half, :] = second[head:head + 1, cols]
    pl.semaphore_wait(barrier, steps + 1)
    edge.begin()

    depthwise = (first + pltpu.roll(second, ROWS - 1, 0)).astype(jnp.bfloat16)
    load_w.wait()
    key_part = jnp.dot(depthwise[:, :KV], w_ref[0], preferred_element_type=jnp.float32).astype(jnp.bfloat16)
    value_part = jnp.dot(depthwise[:, KV:], w_ref[1], preferred_element_type=jnp.float32).astype(jnp.bfloat16)
    own[:, :KV] = key_part.astype(jnp.float32)
    own[:, KV:] = value_part.astype(jnp.float32)
    for g in range(KVH):
        blocks[me, :, g * HD:(g + 1) * HD] = unit(own[:, g * HD:(g + 1) * HD]).astype(jnp.bfloat16)
    blocks[me, :, KV:] = value_part
    main.begin()

    def queries_of(g):
        own_unit = unit(kvf[g]).astype(jnp.bfloat16).astype(jnp.float32)
        own_value = kvf[KVH + g]
        lane = lax.broadcasted_iota(jnp.int32, (TOK, HD), 1)
        for h in range(g * GROUP, (g + 1) * GROUP):
            rows = slice(h * TOK, (h + 1) * TOK)
            low = unit(q_ref[:, h * HD:(h + 1) * HD].astype(jnp.float32)).astype(jnp.bfloat16)
            qn[rows, :] = low
            score = jnp.sum(low.astype(jnp.float32) * own_unit, axis=1, keepdims=True)
            weight = jnp.exp2(EXP2_SCALE * score)
            acc[rows, :] = weight * own_value
            den[rows, :] = jnp.where(lane == 0, weight, 0.0)

    load_q.wait()
    for k in range(1, steps):
        edge.relay_z(k)
    queries_of(0)
    queries_of(1)
    for k in range(steps):
        edge.relay_y(k)
    queries_of(2)
    queries_of(3)
    for k in range(1, steps):
        main.relay_z(k)
        if k < 4:
            queries_of(3 + k)
    queries_of(7)
    for j in range(2 * steps):
        edge.wait_c(j)

    slot_col = lax.broadcasted_iota(jnp.int32, (pages, 4 * SLOTS * n), 0)
    line = lax.broadcasted_iota(jnp.int32, (pages, 4 * SLOTS * n), 1)
    kind = line % 8
    line_slot = (line // 8) * SLOTS + (kind // 2) % 2
    page_of_slot = jnp.zeros((pages, 4 * SLOTS * n), jnp.int32)
    page_of_line = jnp.zeros((pages, 4 * SLOTS * n), jnp.int32)
    for s in range(pages):
        page_of_slot = jnp.where(slot_col == s, pt_ref[s], page_of_slot)
        page_of_line = jnp.where(line_slot == s, pt_ref[s], page_of_line)
    take = ((kind < 4) & (slot_col == line_slot)) | ((kind >= 4) & (page_of_line == page_of_slot + 1))
    lines = edges[...].reshape(n * 8, KV)
    for half in range(2):
        pick = jnp.where(take & (kind % 2 == half), 1.0, 0.0)
        row = jnp.dot(pick, lines, preferred_element_type=jnp.float32, precision=lax.Precision.HIGHEST)
        part = jnp.dot(row.astype(jnp.bfloat16), w_ref[half], preferred_element_type=jnp.float32)
        part = part.astype(jnp.bfloat16).astype(jnp.float32)
        tails_comp[:, half * KV:(half + 1) * KV] = part
        if half == 0:
            for g in range(KVH):
                cols = slice(g * HD, (g + 1) * HD)
                tails[:, cols] = unit(part[:, cols]).astype(jnp.bfloat16).astype(jnp.float32)
        else:
            tails[:, KV:] = part

    row_id = lax.broadcasted_iota(jnp.int32, (ROWS, 2 * KV), 0)

    def with_tails(block, table, b):
        t0 = table[pl.ds(SLOTS * b, 1), :]
        t1 = table[pl.ds(SLOTS * b + 1, 1), :]
        return jnp.where(row_id == CR - 1, t0, jnp.where(row_id == 2 * CR - 1, t1, block)).astype(jnp.bfloat16)

    tier_ref[...] = with_tails(own[...], tails_comp, me)

    token = lax.broadcasted_iota(jnp.int32, (TOK, 1), 0)
    page_here = jnp.where(token < PAGE, pt_ref[SLOTS * me], pt_ref[SLOTS * me + 1])
    position = page_here * PAGE + token % PAGE
    doc_start = jnp.zeros((TOK, 1), jnp.int32)
    end = jnp.int32(0)
    for d in range(dl_ref.shape[0]):
        end = end + dl_ref[d]
        doc_start = doc_start + jnp.where(end <= position, dl_ref[d], 0)

    def attend(members):
        count = len(members) * ROWS
        lane = lax.broadcasted_iota(jnp.int32, (1, count), 1)
        page_of = jnp.zeros((1, count), jnp.int32)
        for i, b in enumerate(members):
            keys[i * ROWS:(i + 1) * ROWS, :] = with_tails(blocks[b].astype(jnp.float32), tails, b)
            for s in range(SLOTS):
                page_of = jnp.where(lane // CR == i * SLOTS + s, pt_ref[SLOTS * b + s], page_of)
        start = STRIDE * (page_of * CR + lane % CR)
        seen = jnp.where((start >= doc_start) & (start + KERNEL - 1 < position), 1.0, 0.0)
        for g in range(KVH):
            rows = slice(g * GROUP * TOK, (g + 1) * GROUP * TOK)
            key_block = keys[:count, g * HD:(g + 1) * HD]
            value_block = keys[:count, KV + g * HD:KV + (g + 1) * HD]
            score = lax.dot_general(qn[rows, :], key_block, (((1,), (1,)), ((), ())),
                                    preferred_element_type=jnp.float32)
            weight = jnp.exp2(EXP2_SCALE * score).reshape(GROUP, TOK, count) * seen[None]
            weight = weight.reshape(GROUP * TOK, count)
            acc[rows, :] += jnp.dot(weight.astype(jnp.bfloat16), value_block, preferred_element_type=jnp.float32)
            total = den[rows, :]
            for i in range(count // HD):
                total = total + weight[:, i * HD:(i + 1) * HD]
            den[rows, :] = total

    near = [main.origin(k, main.y, c) for k in range(steps) for c in (main.c, 1 - main.c)]
    far = [main.origin(k, 1 - main.y, c) for k in range(steps) for c in (main.c, 1 - main.c)]
    for j in range(steps):
        main.wait_c(j)
    for a in range(0, len(near), CHUNK_BLOCKS):
        attend(near[a:a + CHUNK_BLOCKS])
    for k in range(steps):
        main.relay_y(k)
    for k in range(steps):
        main.wait_c(steps + k)
    for a in range(0, len(far), CHUNK_BLOCKS):
        attend(far[a:a + CHUNK_BLOCKS])
    for h in range(QH):
        rows = slice(h * TOK, (h + 1) * TOK)
        total = jnp.sum(den[rows, :], axis=1, keepdims=True)
        att_ref[:, h * HD:(h + 1) * HD] = (acc[rows, :] * (1.0 / total)).astype(jnp.bfloat16)
    edge.finish()
    main.finish()


def shards(n, queries, keys_values, depth_kernel, point_weight, page_table, doc_lengths):
    pages = page_table.shape[0]
    steps = n // 4
    vmem = pl.BlockSpec(memory_space=pltpu.VMEM)
    hbm = pl.BlockSpec(memory_space=pl.ANY)
    smem = pl.BlockSpec(memory_space=pltpu.SMEM)
    dma = pltpu.SemaphoreType.DMA
    spread = [dma((steps,)), dma((steps,)), dma((steps,)), dma((steps,)), dma((2 * steps,)), dma((2 * steps,))]
    return pl.pallas_call(
        functools.partial(kernel, n, pages),
        out_shape=(jax.ShapeDtypeStruct((TOK, QH * HD), jnp.bfloat16),
                   jax.ShapeDtypeStruct((ROWS, 2 * KV), jnp.bfloat16)),
        in_specs=[hbm, vmem, vmem, hbm, smem, smem],
        out_specs=(vmem, vmem),
        scratch_shapes=[
            pltpu.VMEM((TOK, QH * HD), jnp.bfloat16),
            pltpu.VMEM((2, KV, KV), jnp.bfloat16),
            pltpu.VMEM((2 * KVH, TOK, HD), jnp.float32),
            pltpu.VMEM((n, 8, KV), jnp.float32),
            pltpu.VMEM((n, ROWS, 2 * KV), jnp.bfloat16),
            pltpu.VMEM((ROWS, 2 * KV), jnp.float32),
            pltpu.VMEM((QH * TOK, HD), jnp.bfloat16),
            pltpu.VMEM((QH * TOK, HD), jnp.float32),
            pltpu.VMEM((QH * TOK, HD), jnp.float32),
            pltpu.VMEM((pages, 2 * KV), jnp.float32),
            pltpu.VMEM((pages, 2 * KV), jnp.float32),
            pltpu.VMEM((CHUNK_BLOCKS * ROWS, 2 * KV), jnp.bfloat16),
            dma((2,)),
        ] + spread + spread,
        compiler_params=pltpu.CompilerParams(collective_id=0, has_side_effects=True),
    )(queries, keys_values, depth_kernel, point_weight, page_table, doc_lengths)


def solution(mesh):
    placed = (P(("grp", "ctx"), None), P(("grp", "ctx"), None), P(), P(), P("grp"), P("grp"))
    return jax.shard_map(
        functools.partial(shards, mesh.shape["ctx"]),
        mesh=mesh,
        in_specs=placed,
        out_specs=(P(("grp", "ctx"), None), P(("grp", "ctx"), None)),
        check_vma=False,
    )
```

time: 103 us -> 35.2 us (0.34)
  other arithmetic: 32.8 us -> 0 us
  Pallas kernels: 0 us -> 30.1 us
  blocking collectives: 24.5 us -> 0 us
  local copies, waits for them, and re-layouts: 19.2 us -> 3.85 us
  between operations: 14.4 us -> 0.64 us
  matrix products: 7.46 us -> 0 us
  waiting for transfers between devices: 3.93 us -> 0 us
    pallas_call x0 -> x1, Pallas kernels: none -> 30.1 us  [shards(): pl.pallas_call(functools.partial(kernel, n, pages), out_shape=(jax.ShapeD...]
    all_gather x1 -> x0, blocking collectives: 24.5 us -> none  [shards(): gathered = lax.all_gather(edge_rows, 'ctx', axis=0, tiled=True)]
    sub x1 -> x0, other arithmetic: 15.5 us -> none  [add_block(): row_start[None, :] + KERNEL - 1 < position[:, None]]
    dot_general x5 -> x0, matrix products: 7.46 us -> none  [the longest x1 2.21 us: shards(): jnp.dot(depthwise[:, kv_width:], point_weight[1], preferred_element_type=...]
    gather x28 -> x0, other arithmetic: 5.34 us -> none  [the longest x26 5.33 us: add_block(): jnp.take(page_table, slot_index) * rows_page + row_index % rows_page]
    reduce_sum x5 -> x0, other arithmetic: 4.05 us -> none  [the longest x3 3.12 us: unit_rows(): factor = lax.rsqrt(jnp.mean(pieces * pieces, axis=2, keepdims=True) + 1e-06)]
    all_gather x1 -> x0, waiting for transfers between devices: 3.92 us -> none  [shards(): whole_tier = lax.all_gather(compressed, 'ctx', axis=0, tiled=True)]
    unnamed x2 -> x0, other arithmetic: 3.37 us -> none
  transfers between devices with their start and end apart: 1 -> 0, of which waited for: 1 -> 0; matrix products, arithmetic and copies ran while one was open for 33% -> 0% of each run, Pallas kernels for 0% -> 0%
where the time goes in v1:
time: 35.2 us; the launch traced here: 34.6 us
  Pallas kernels  30.1 us (86%)
  local copies, waits for them, and re-layouts  3.85 us (11%)
  between operations  0.64 us (2%)
    pallas_call x1, Pallas kernels, shards(): pl.pallas_call(functools.partial(kernel, n, pages), out_shape=(jax.ShapeD...  30.1 us
    unnamed x2, local copies, waits for them, and re-layouts  3.85 us

profile of v1, /device:TPU:1, one launch (start us, length us, event | category | flops | bytes accessed | tf_op | source)
XLA Modules:
  0.0 34.6 jit_solution(17504858135877099236)
XLA Ops:
  0.6 30.1 %shard_map.77 = (bf16[128,4096]{1,0:T(8,128)(2,1)}, bf16[32,2048]{1,0:T(8,128)(2,1)}) custom-call(bf16[128,4096]{1,0:T(8,128)(2,1)} %q_hbm.1, bf16[128,2048]{1,0:T(8,128)(2,1)} %kv_ref.1, f32[8,2048]{1,0:T(8,128)} %dk_ref.1, bf16[2,1024,1024]{2,1,0:T(8,128)(2,1)} %w_hbm.1, s32[32]{0:T(128)} %pt_ref.1, s32[4]{0:T(128)} %dl_ref.1), custom_call_target="tpu_custom_call" | custom-call | tf_op jit(solution)/shard_map/pallas_call | solution.py:279
  30.7 2.3 %copy.10 = bf16[128,4096]{1,0:T(8,128)(2,1)} copy(bf16[128,4096]{1,0:T(8,128)(2,1)} %get-tuple-element.4) | data formatting | bytes 2097152
  33.0 1.6 %copy.11 = bf16[32,2048]{1,0:T(8,128)(2,1)} copy(bf16[32,2048]{1,0:T(8,128)(2,1)} %get-tuple-element.5) | data formatting | bytes 262144

commit v2 on v1

--- a/solution.py
+++ b/solution.py
@@ -22,6 +22,8 @@
 ROWS = SLOTS * CR
 TOK = SLOTS * PAGE
 CHUNK_BLOCKS = 8
+PIECES = 4
+PIECE = 2 * KV // PIECES
 MESH = pl.DeviceIdType.MESH
 
 
@@ -100,23 +102,106 @@
             self.c_out(j).wait_send()
 
 
+class Ring:
+    def __init__(self, buf, chips, r_send, r_recv, l_send, l_recv, c_send, c_recv):
+        self.buf, self.chips, self.half = buf, chips, chips // 2
+        self.sems = dict(r=(r_send, r_recv), l=(l_send, l_recv), c=(c_send, c_recv))
+        me = lax.axis_index("ctx")
+        self.me, self.c = me, lax.rem(me, 2)
+        self.snake = chips <= 8
+        chip = me // 2
+        if self.snake:
+            z, y = chip // 2, lax.rem(chip, 2)
+            chip = z + y * (chips - 1 - 2 * z)
+        self.r = chip
+
+    def at(self, d, other=False):
+        r = lax.rem(self.r + d + self.chips, self.chips)
+        if self.snake:
+            high = r // self.half
+            r = 2 * (r + high * (self.chips - 1 - 2 * r)) + high
+        return r * 2 + (1 - self.c if other else self.c)
+
+    def copy(self, kind, i, origin, p, target):
+        send, recv = self.sems[kind]
+        piece = self.buf.at[origin, p]
+        return pltpu.make_async_remote_copy(
+            src_ref=piece, dst_ref=piece, send_sem=send.at[i], recv_sem=recv.at[i],
+            device_id={"ctx": target}, device_id_type=MESH)
+
+    def right(self, d, p, arriving=False):
+        return self.copy("r", (d - arriving) * PIECES + p, self.at(-d), p, self.at(1))
+
+    def left(self, d, p, arriving=False):
+        return self.copy("l", (d - arriving) * PIECES + p, self.at(d), p, self.at(-1))
+
+    def core(self, d, p, arriving=False):
+        return self.copy("c", (d % self.chips) * PIECES + p, self.at(d, arriving), p, self.at(0, True))
+
+    def goes_right(self, d, p):
+        return d < self.half - 1 or (d == self.half - 1 and p % 2 == 0)
+
+    def goes_left(self, d, p):
+        return d < self.half - 1 or (d == self.half - 1 and p % 2 == 1)
+
+    def begin(self, p):
+        if self.goes_right(0, p):
+            self.right(0, p).start()
+        if self.goes_left(0, p):
+            self.left(0, p).start()
+        self.core(0, p).start()
+
+    def relay(self, d, p):
+        if self.goes_right(d - 1, p):
+            self.right(d, p, True).wait_recv()
+            if self.goes_right(d, p):
+                self.right(d, p).start()
+            self.core(-d, p).start()
+        if self.goes_left(d - 1, p):
+            self.left(d, p, True).wait_recv()
+            if self.goes_left(d, p):
+                self.left(d, p).start()
+            self.core(d, p).start()
+
+    def wait_core(self, d):
+        for p in range(PIECES):
+            self.core(d, p, True).wait_recv()
+
+    def finish(self):
+        for d in range(self.half):
+            for p in range(PIECES):
+                if self.goes_right(d, p):
+                    self.right(d, p).wait_send()
+                if self.goes_left(d, p):
+                    self.left(d, p).wait_send()
+        for d in range(self.chips):
+            for p in range(PIECES):
+                self.core(d, p).wait_send()
+
+
 def kernel(n, pages, q_hbm, kv_ref, dk_ref, w_hbm, pt_ref, dl_ref, att_ref, tier_ref,
            q_ref, w_ref, kvf, edges, blocks, own, qn, acc, den, tails, tails_comp, keys,
-           load_sem, ez_s, ez_r, ey_s, ey_r, ec_s, ec_r, mz_s, mz_r, my_s, my_r, mc_s, mc_r):
+           load_sem, ez_s, ez_r, ey_s, ey_r, ec_s, ec_r, *ring_sems):
     steps = n // 4
     me = lax.axis_index("ctx")
-    load_w = pltpu.make_async_copy(w_hbm, w_ref, load_sem.at[0])
-    load_q = pltpu.make_async_copy(q_hbm, q_ref, load_sem.at[1])
-    load_w.start()
+    halves = [1 - p // 2 for p in range(PIECES)]
+    inside = [slice(p % 2 * PIECE, (p % 2 + 1) * PIECE) for p in range(PIECES)]
+    across = [slice(half * KV + p % 2 * PIECE, half * KV + (p % 2 + 1) * PIECE) for p, half in enumerate(halves)]
+    load_w = [pltpu.make_async_copy(w_hbm.at[halves[p], :, inside[p]], w_ref.at[p], load_sem.at[p]) for p in range(PIECES)]
+    load_q = pltpu.make_async_copy(q_hbm, q_ref, load_sem.at[PIECES])
+    for load in load_w:
+        load.start()
     load_q.start()
     edge = Spread(edges, ez_s, ez_r, ey_s, ey_r, ec_s, ec_r, steps)
-    main = Spread(blocks, mz_s, mz_r, my_s, my_r, mc_s, mc_r, steps)
+    main = Ring(blocks, n // 2, *ring_sems)
 
     barrier = pltpu.get_barrier_semaphore()
     for k in range(1, steps):
         pl.semaphore_signal(barrier, inc=1, device_id={"ctx": edge.z_target(k)}, device_id_type=MESH)
     pl.semaphore_signal(barrier, inc=1, device_id={"ctx": edge.index(edge.z, 1 - edge.y, edge.c)}, device_id_type=MESH)
     pl.semaphore_signal(barrier, inc=1, device_id={"ctx": edge.index(edge.z, edge.y, 1 - edge.c)}, device_id_type=MESH)
+    for side in (-1, 1):
+        pl.semaphore_signal(barrier, inc=1, device_id={"ctx": main.at(side)}, device_id_type=MESH)
 
     firsts, seconds = [], []
     for t in range(2 * KVH):
@@ -138,19 +223,23 @@
             cols = slice(half * KV, (half + 1) * KV)
             edges[me, 2 * s + half:2 * s + half + 1, :] = first[last:last + 1, cols]
             edges[me, 4 + 2 * s + half:5 + 2 * s + half, :] = second[head:head + 1, cols]
-    pl.semaphore_wait(barrier, steps + 1)
+    pl.semaphore_wait(barrier, steps + 3)
     edge.begin()
 
     depthwise = (first + pltpu.roll(second, ROWS - 1, 0)).astype(jnp.bfloat16)
-    load_w.wait()
-    key_part = jnp.dot(depthwise[:, :KV], w_ref[0], preferred_element_type=jnp.float32).astype(jnp.bfloat16)
-    value_part = jnp.dot(depthwise[:, KV:], w_ref[1], preferred_element_type=jnp.float32).astype(jnp.bfloat16)
-    own[:, :KV] = key_part.astype(jnp.float32)
-    own[:, KV:] = value_part.astype(jnp.float32)
-    for g in range(KVH):
-        blocks[me, :, g * HD:(g + 1) * HD] = unit(own[:, g * HD:(g + 1) * HD]).astype(jnp.bfloat16)
-    blocks[me, :, KV:] = value_part
-    main.begin()
+    for p in range(PIECES):
+        load_w[p].wait()
+        taken = depthwise[:, halves[p] * KV:(halves[p] + 1) * KV]
+        part = jnp.dot(taken, w_ref[p], preferred_element_type=jnp.float32).astype(jnp.bfloat16)
+        wide = part.astype(jnp.float32)
+        own[:, across[p]] = wide
+        if halves[p]:
+            blocks[me, p] = part
+        else:
+            for g in range(PIECE // HD):
+                cols = slice(g * HD, (g + 1) * HD)
+                blocks[me, p, :, cols] = unit(wide[:, cols]).astype(jnp.bfloat16)
+        main.begin(p)
 
     def queries_of(g):
         own_unit = unit(kvf[g]).astype(jnp.bfloat16).astype(jnp.float32)
@@ -168,17 +257,16 @@
     load_q.wait()
     for k in range(1, steps):
         edge.relay_z(k)
-    queries_of(0)
-    queries_of(1)
+    for g in range(3):
+        queries_of(g)
     for k in range(steps):
         edge.relay_y(k)
-    queries_of(2)
-    queries_of(3)
-    for k in range(1, steps):
-        main.relay_z(k)
-        if k < 4:
-            queries_of(3 + k)
+    for p in range(PIECES):
+        main.relay(1, p)
+        queries_of(3 + p)
     queries_of(7)
+    for p in range(PIECES):
+        main.relay(2, p)
     for j in range(2 * steps):
         edge.wait_c(j)
 
@@ -193,27 +281,32 @@
         page_of_line = jnp.where(line_slot == s, pt_ref[s], page_of_line)
     take = ((kind < 4) & (slot_col == line_slot)) | ((kind >= 4) & (page_of_line == page_of_slot + 1))
     lines = edges[...].reshape(n * 8, KV)
+    rows_last = []
     for half in range(2):
         pick = jnp.where(take & (kind % 2 == half), 1.0, 0.0)
         row = jnp.dot(pick, lines, preferred_element_type=jnp.float32, precision=lax.Precision.HIGHEST)
-        part = jnp.dot(row.astype(jnp.bfloat16), w_ref[half], preferred_element_type=jnp.float32)
+        rows_last.append(row.astype(jnp.bfloat16))
+    for p in range(PIECES):
+        part = jnp.dot(rows_last[halves[p]], w_ref[p], preferred_element_type=jnp.float32)
         part = part.astype(jnp.bfloat16).astype(jnp.float32)
-        tails_comp[:, half * KV:(half + 1) * KV] = part
-        if half == 0:
-            for g in range(KVH):
+        tails_comp[:, across[p]] = part
+        if halves[p]:
+            tails[:, across[p]] = part
+        else:
+            for g in range(PIECE // HD):
                 cols = slice(g * HD, (g + 1) * HD)
-                tails[:, cols] = unit(part[:, cols]).astype(jnp.bfloat16).astype(jnp.float32)
-        else:
-            tails[:, KV:] = part
-
-    row_id = lax.broadcasted_iota(jnp.int32, (ROWS, 2 * KV), 0)
-
-    def with_tails(block, table, b):
-        t0 = table[pl.ds(SLOTS * b, 1), :]
-        t1 = table[pl.ds(SLOTS * b + 1, 1), :]
+                tails[:, p % 2 * PIECE + g * HD:p % 2 * PIECE + (g + 1) * HD] = (
+                    unit(part[:, cols]).astype(jnp.bfloat16).astype(jnp.float32))
+
+    row_id = lax.broadcasted_iota(jnp.int32, (ROWS, PIECE), 0)
+
+    def with_tails(block, table, b, cols):
+        t0 = table[pl.ds(SLOTS * b, 1), cols]
+        t1 = table[pl.ds(SLOTS * b + 1, 1), cols]
         return jnp.where(row_id == CR - 1, t0, jnp.where(row_id == 2 * CR - 1, t1, block)).astype(jnp.bfloat16)
 
-    tier_ref[...] = with_tails(own[...], tails_comp, me)
+    for p in range(PIECES):
+        tier_ref[:, across[p]] = with_tails(own[:, across[p]], tails_comp, me, across[p])
 
     token = lax.broadcasted_iota(jnp.int32, (TOK, 1), 0)
     page_here = jnp.where(token < PAGE, pt_ref[SLOTS * me], pt_ref[SLOTS * me + 1])
@@ -229,7 +322,8 @@
         lane = lax.broadcasted_iota(jnp.int32, (1, count), 1)
         page_of = jnp.zeros((1, count), jnp.int32)
         for i, b in enumerate(members):
-            keys[i * ROWS:(i + 1) * ROWS, :] = with_tails(blocks[b].astype(jnp.float32), tails, b)
+            for p in range(PIECES):
+                keys[i * ROWS:(i + 1) * ROWS, across[p]] = with_tails(blocks[b, p].astype(jnp.float32), tails, b, across[p])
             for s in range(SLOTS):
                 page_of = jnp.where(lane // CR == i * SLOTS + s, pt_ref[SLOTS * b + s], page_of)
         start = STRIDE * (page_of * CR + lane % CR)
@@ -248,18 +342,21 @@
                 total = total + weight[:, i * HD:(i + 1) * HD]
             den[rows, :] = total
 
-    near = [main.origin(k, main.y, c) for k in range(steps) for c in (main.c, 1 - main.c)]
-    far = [main.origin(k, 1 - main.y, c) for k in range(steps) for c in (main.c, 1 - main.c)]
-    for j in range(steps):
-        main.wait_c(j)
-    for a in range(0, len(near), CHUNK_BLOCKS):
-        attend(near[a:a + CHUNK_BLOCKS])
-    for k in range(steps):
-        main.relay_y(k)
-    for k in range(steps):
-        main.wait_c(steps + k)
-    for a in range(0, len(far), CHUNK_BLOCKS):
-        attend(far[a:a + CHUNK_BLOCKS])
+    half = n // 4
+    ds = [0]
+    for d in range(1, half):
+        ds += [-d, d]
+    ds.append(half)
+    relayed, chips_of_chunk = 2, CHUNK_BLOCKS // 2
+    for a in range(0, len(ds), chips_of_chunk):
+        part = ds[a:a + chips_of_chunk]
+        while relayed < max(abs(d) for d in part):
+            relayed += 1
+            for p in range(PIECES):
+                main.relay(relayed, p)
+        for d in part:
+            main.wait_core(d)
+        attend([main.at(d, other) for d in part for other in (False, True)])
     for h in range(QH):
         rows = slice(h * TOK, (h + 1) * TOK)
         total = jnp.sum(den[rows, :], axis=1, keepdims=True)
@@ -276,6 +373,7 @@
     smem = pl.BlockSpec(memory_space=pltpu.SMEM)
     dma = pltpu.SemaphoreType.DMA
     spread = [dma((steps,)), dma((steps,)), dma((steps,)), dma((steps,)), dma((2 * steps,)), dma((2 * steps,))]
+    ring = [dma((steps * PIECES,))] * 4 + [dma((n // 2 * PIECES,))] * 2
     return pl.pallas_call(
         functools.partial(kernel, n, pages),
         out_shape=(jax.ShapeDtypeStruct((TOK, QH * HD), jnp.bfloat16),
@@ -284,10 +382,10 @@
         out_specs=(vmem, vmem),
         scratch_shapes=[
             pltpu.VMEM((TOK, QH * HD), jnp.bfloat16),
-            pltpu.VMEM((2, KV, KV), jnp.bfloat16),
+            pltpu.VMEM((PIECES, KV, PIECE), jnp.bfloat16),
             pltpu.VMEM((2 * KVH, TOK, HD), jnp.float32),
             pltpu.VMEM((n, 8, KV), jnp.float32),
-            pltpu.VMEM((n, ROWS, 2 * KV), jnp.bfloat16),
+            pltpu.VMEM((n, PIECES, ROWS, PIECE), jnp.bfloat16),
             pltpu.VMEM((ROWS, 2 * KV), jnp.float32),
             pltpu.VMEM((QH * TOK, HD), jnp.bfloat16),
             pltpu.VMEM((QH * TOK, HD), jnp.float32),
@@ -295,8 +393,8 @@
             pltpu.VMEM((pages, 2 * KV), jnp.float32),
             pltpu.VMEM((pages, 2 * KV), jnp.float32),
             pltpu.VMEM((CHUNK_BLOCKS * ROWS, 2 * KV), jnp.bfloat16),
-            dma((2,)),
-        ] + spread + spread,
+            dma((PIECES + 1,)),
+        ] + spread + ring,
         compiler_params=pltpu.CompilerParams(collective_id=0, has_side_effects=True),
     )(queries, keys_values, depth_kernel, point_weight, page_table, doc_lengths)
 

time: 35.2 us -> 35.2 us (level); the launches traced: 34.6 us -> 35 us
  Pallas kernels: 30.1 us -> 30.6 us
    pallas_call x1, Pallas kernels: 30.1 us -> 30.6 us  [shards(): pl.pallas_call(functools.partial(kernel, n, pages), out_shape=(jax.ShapeD...]
where the time goes in v2:
time: 35.2 us; the launch traced here: 35 us
  Pallas kernels  30.6 us (87%)
  local copies, waits for them, and re-layouts  3.85 us (11%)
  between operations  0.64 us (2%)
    pallas_call x1, Pallas kernels, shards(): pl.pallas_call(functools.partial(kernel, n, pages), out_shape=(jax.ShapeD...  30.6 us
    unnamed x2, local copies, waits for them, and re-layouts  3.85 us

profile of v2, /device:TPU:1, one launch (start us, length us, event | category | flops | bytes accessed | tf_op | source)
XLA Modules:
  0.0 35.0 jit_solution(295997012980335111)
XLA Ops:
  0.6 30.6 %shard_map.77 = (bf16[128,4096]{1,0:T(8,128)(2,1)}, bf16[32,2048]{1,0:T(8,128)(2,1)}) custom-call(bf16[128,4096]{1,0:T(8,128)(2,1)} %q_hbm.1, bf16[128,2048]{1,0:T(8,128)(2,1)} %kv_ref.1, f32[8,2048]{1,0:T(8,128)} %dk_ref.1, bf16[2,1024,1024]{2,1,0:T(8,128)(2,1)} %w_hbm.1, s32[32]{0:T(128)} %pt_ref.1, s32[4]{0:T(128)} %dl_ref.1), custom_call_target="tpu_custom_call" | custom-call | tf_op jit(solution)/shard_map/pallas_call | solution.py:377
  31.2 2.3 %copy.10 = bf16[128,4096]{1,0:T(8,128)(2,1)} copy(bf16[128,4096]{1,0:T(8,128)(2,1)} %get-tuple-element.4) | data formatting | bytes 2097152
  33.5 1.6 %copy.11 = bf16[32,2048]{1,0:T(8,128)(2,1)} copy(bf16[32,2048]{1,0:T(8,128)(2,1)} %get-tuple-element.5) | data formatting | bytes 262144

commit v3 on v2

--- a/solution.py
+++ b/solution.py
@@ -179,8 +179,8 @@
                 self.core(d, p).wait_send()
 
 
-def kernel(n, pages, q_hbm, kv_ref, dk_ref, w_hbm, pt_ref, dl_ref, att_ref, tier_ref,
-           q_ref, w_ref, kvf, edges, blocks, own, qn, acc, den, tails, tails_comp, keys,
+def kernel(n, pages, q_hbm, kv_hbm, dk_hbm, w_hbm, pt_ref, dl_ref, att_ref, tier_ref,
+           q_ref, kv_ref, dk_ref, w_ref, kvf, edges, blocks, own, qn, acc, den, tails, tails_comp, keys,
            load_sem, ez_s, ez_r, ey_s, ey_r, ec_s, ec_r, *ring_sems):
     steps = n // 4
     me = lax.axis_index("ctx")
@@ -189,7 +189,9 @@
     across = [slice(half * KV + p % 2 * PIECE, half * KV + (p % 2 + 1) * PIECE) for p, half in enumerate(halves)]
     load_w = [pltpu.make_async_copy(w_hbm.at[halves[p], :, inside[p]], w_ref.at[p], load_sem.at[p]) for p in range(PIECES)]
     load_q = pltpu.make_async_copy(q_hbm, q_ref, load_sem.at[PIECES])
-    for load in load_w:
+    load_kv = pltpu.make_async_copy(kv_hbm, kv_ref, load_sem.at[PIECES + 1])
+    load_dk = pltpu.make_async_copy(dk_hbm, dk_ref, load_sem.at[PIECES + 2])
+    for load in [load_kv, load_dk] + load_w:
         load.start()
     load_q.start()
     edge = Spread(edges, ez_s, ez_r, ey_s, ey_r, ec_s, ec_r, steps)
@@ -203,6 +205,8 @@
     for side in (-1, 1):
         pl.semaphore_signal(barrier, inc=1, device_id={"ctx": main.at(side)}, device_id_type=MESH)
 
+    load_kv.wait()
+    load_dk.wait()
     firsts, seconds = [], []
     for t in range(2 * KVH):
         cols = slice(t * HD, (t + 1) * HD)
@@ -255,18 +259,21 @@
             den[rows, :] = jnp.where(lane == 0, weight, 0.0)
 
     load_q.wait()
+    queries_of(0)
+    queries_of(1)
     for k in range(1, steps):
         edge.relay_z(k)
-    for g in range(3):
-        queries_of(g)
+    for p in range(PIECES):
+        main.relay(1, p)
+        queries_of(2 + p)
     for k in range(steps):
         edge.relay_y(k)
     for p in range(PIECES):
-        main.relay(1, p)
-        queries_of(3 + p)
+        main.relay(2, p)
+    queries_of(6)
     queries_of(7)
     for p in range(PIECES):
-        main.relay(2, p)
+        main.relay(3, p)
     for j in range(2 * steps):
         edge.wait_c(j)
 
@@ -347,7 +354,7 @@
     for d in range(1, half):
         ds += [-d, d]
     ds.append(half)
-    relayed, chips_of_chunk = 2, CHUNK_BLOCKS // 2
+    relayed, chips_of_chunk = 3, CHUNK_BLOCKS // 2
     for a in range(0, len(ds), chips_of_chunk):
         part = ds[a:a + chips_of_chunk]
         while relayed < max(abs(d) for d in part):
@@ -365,23 +372,35 @@
     main.finish()
 
 
+def place(att_in, tier_in, att_out, tier_out, sems):
+    first = pltpu.make_async_copy(att_in, att_out, sems.at[0])
+    second = pltpu.make_async_copy(tier_in, tier_out, sems.at[1])
+    first.start()
+    second.start()
+    first.wait()
+    second.wait()
+
+
 def shards(n, queries, keys_values, depth_kernel, point_weight, page_table, doc_lengths):
     pages = page_table.shape[0]
     steps = n // 4
+    held = pl.BlockSpec(memory_space=pltpu.HBM)
     vmem = pl.BlockSpec(memory_space=pltpu.VMEM)
     hbm = pl.BlockSpec(memory_space=pl.ANY)
     smem = pl.BlockSpec(memory_space=pltpu.SMEM)
     dma = pltpu.SemaphoreType.DMA
     spread = [dma((steps,)), dma((steps,)), dma((steps,)), dma((steps,)), dma((2 * steps,)), dma((2 * steps,))]
     ring = [dma((steps * PIECES,))] * 4 + [dma((n // 2 * PIECES,))] * 2
-    return pl.pallas_call(
+    outs = pl.pallas_call(
         functools.partial(kernel, n, pages),
         out_shape=(jax.ShapeDtypeStruct((TOK, QH * HD), jnp.bfloat16),
                    jax.ShapeDtypeStruct((ROWS, 2 * KV), jnp.bfloat16)),
-        in_specs=[hbm, vmem, vmem, hbm, smem, smem],
+        in_specs=[held, held, held, held, smem, smem],
         out_specs=(vmem, vmem),
         scratch_shapes=[
             pltpu.VMEM((TOK, QH * HD), jnp.bfloat16),
+            pltpu.VMEM((TOK, 2 * KV), jnp.bfloat16),
+            pltpu.VMEM((KERNEL, 2 * KV), jnp.float32),
             pltpu.VMEM((PIECES, KV, PIECE), jnp.bfloat16),
             pltpu.VMEM((2 * KVH, TOK, HD), jnp.float32),
             pltpu.VMEM((n, 8, KV), jnp.float32),
@@ -393,10 +412,18 @@
             pltpu.VMEM((pages, 2 * KV), jnp.float32),
             pltpu.VMEM((pages, 2 * KV), jnp.float32),
             pltpu.VMEM((CHUNK_BLOCKS * ROWS, 2 * KV), jnp.bfloat16),
-            dma((PIECES + 1,)),
+            dma((PIECES + 3,)),
         ] + spread + ring,
         compiler_params=pltpu.CompilerParams(collective_id=0, has_side_effects=True),
     )(queries, keys_values, depth_kernel, point_weight, page_table, doc_lengths)
+    return pl.pallas_call(
+        place,
+        out_shape=[jax.ShapeDtypeStruct(x.shape, x.dtype) for x in outs],
+        in_specs=[vmem, vmem],
+        out_specs=[hbm, hbm],
+        scratch_shapes=[dma((2,))],
+        compiler_params=pltpu.CompilerParams(vmem_limit_bytes=4 << 20),
+    )(*outs)
 
 
 def solution(mesh):

time: 35.2 us -> 31.9 us (0.906)
  local copies, waits for them, and re-layouts: 3.85 us -> 2.12 us
  Pallas kernels: 30.6 us -> 29 us
    pallas_call x1, Pallas kernels: 30.6 us -> 28 us  [shards(): pl.pallas_call(functools.partial(kernel, n, pages), out_shape=(jax.ShapeD...]
    unnamed x2 -> x4, local copies, waits for them, and re-layouts: 3.85 us -> 2.12 us
    pallas_call x0 -> x1, Pallas kernels: none -> 1.02 us  [shards(): pl.pallas_call(place, out_shape=[jax.ShapeDtypeStruct(x.shape, x.dtype) f...]
where the time goes in v3:
time: 31.9 us; the launch traced here: 31.7 us
  Pallas kernels  29 us (91%)
  local copies, waits for them, and re-layouts  2.12 us (7%)
  between operations  0.65 us (2%)
    pallas_call x1, Pallas kernels, shards(): pl.pallas_call(functools.partial(kernel, n, pages), out_shape=(jax.ShapeD...  28 us
    unnamed x4, local copies, waits for them, and re-layouts  2.12 us
    pallas_call x1, Pallas kernels, shards(): pl.pallas_call(place, out_shape=[jax.ShapeDtypeStruct(x.shape, x.dtype) f...  1.02 us

profile of v3, /device:TPU:1, one launch (start us, length us, event | category | flops | bytes accessed | tf_op | source)
XLA Modules:
  0.0 31.7 jit_solution(11470392188519158002)
XLA Ops:
  0.6 28.0 %shard_map.77 = (bf16[128,4096]{1,0:T(8,128)(2,1)}, bf16[32,2048]{1,0:T(8,128)(2,1)}) custom-call(bf16[128,4096]{1,0:T(8,128)(2,1)} %q_hbm.1, bf16[128,2048]{1,0:T(8,128)(2,1)} %kv_hbm.1, f32[8,2048]{1,0:T(8,128)} %dk_hbm.1, bf16[2,1024,1024]{2,1,0:T(8,128)(2,1)} %w_hbm.1, s32[32]{0:T(128)} %pt_ref.1, s32[4]{0:T(128)} %dl_ref.1), custom_call_target="tpu_custom_call" | custom-call | tf_op jit(solution)/shard_map/pallas_call | solution.py:394
  28.6 0.0 copy-start
  28.6 1.2 %copy-done = bf16[128,4096]{1,0:T(8,128)(2,1)S(1)} copy-done((bf16[128,4096]{1,0:T(8,128)(2,1)S(1)}, bf16[128,4096]{1,0:T(8,128)(2,1)}, u32[]{:S(2)}) %copy-start) | copy-done | bytes 1048600
  29.8 0.0 copy-start.1
  29.8 0.9 %copy-done.1 = bf16[32,2048]{1,0:T(8,128)(2,1)S(1)} copy-done((bf16[32,2048]{1,0:T(8,128)(2,1)S(1)}, bf16[32,2048]{1,0:T(8,128)(2,1)}, u32[]{:S(2)}) %copy-start.1) | copy-done | bytes 131096
  30.7 1.0 %shard_map.78 = (bf16[128,4096]{1,0:T(8,128)(2,1)}, bf16[32,2048]{1,0:T(8,128)(2,1)}) custom-call(bf16[128,4096]{1,0:T(8,128)(2,1)S(1)} %copy-done, bf16[32,2048]{1,0:T(8,128)(2,1)S(1)} %copy-done.1), custom_call_target="tpu_custom_call" | custom-call | tf_op jit(solution)/shard_map/pallas_call | solution.py:419
Async XLA Ops:
  28.6 1.2 %copy-start = (bf16[128,4096]{1,0:T(8,128)(2,1)S(1)}, bf16[128,4096]{1,0:T(8,128)(2,1)}, u32[]{:S(2)}) copy-start(bf16[128,4096]{1,0:T(8,128)(2,1)} %get-tuple-element.4.att_in) | copy-start | bytes 3145732
  29.8 0.9 %copy-start.1 = (bf16[32,2048]{1,0:T(8,128)(2,1)S(1)}, bf16[32,2048]{1,0:T(8,128)(2,1)}, u32[]{:S(2)}) copy-start(bf16[32,2048]{1,0:T(8,128)(2,1)} %get-tuple-element.5.tier_in) | copy-start | bytes 393220
